TPU v7x, 32 devices: a whole 2x2x4 slice. The times are simulated.
32 devices in a mesh: groups: 1, row: 16 (over z, y, core), col: 2 (over x).
Axes of the slice: x: 2, y: 2, z: 4, core: 2. Of those that a mesh axis runs over, the one named last changes fastest.
Arguments:
- pair_grid: bfloat16 [256, 256, 128], P(('groups', 'row'), 'col'), may hold values from -6 to 6
- alignment_pool: bfloat16 [256, 256, 64], P('groups', 'row'), may hold values from -6 to 6
- sample_index: int32 [64], P('groups'), may hold values from 0 to 255
- token_mask: int32 [256], P('groups'), may hold values 0 or 1
- outer_proj: bfloat16 [64, 64], replicated, may hold values from -0.75 to 0.75
- outer_mix: bfloat16 [1024, 128], replicated, may hold values from -0.375 to 0.375
- pair_logit: bfloat16 [128, 8], replicated, may hold values from -1 to 1
- average_proj: bfloat16 [64, 512], replicated, may hold values from -0.75 to 0.75
- average_mix: bfloat16 [256, 64], replicated, may hold values from -0.75 to 0.75
- triangle_proj: bfloat16 [128, 640], replicated, may hold values from -0.5 to 0.5
- triangle_mix: bfloat16 [128, 128], replicated, may hold values from -0.5 to 0.5
- transition_up: bfloat16 [128, 1024], replicated, may hold values from -0.5 to 0.5
- transition_down: bfloat16 [512, 128], replicated, may hold values from -0.25 to 0.25
Outputs:
- pair_next: bfloat16 [256, 256, 128], P(('groups', 'row'), 'col')
- alignment_next: bfloat16 [64, 256, 64], P('groups', 'row')
Inputs may be any that keep to these rules, and one draw needn't show every extreme that they name: `sample_index`: indices into the first dimension of alignment_pool; they may repeat. `token_mask`: 1 marks a real residue, 0 a padded one.
All inputs are finite; a program needn't handle non-finite values.
Results may differ from a plain program's by a relative error of at most 0.008.
Values may be sent and summed in bfloat16 or wider, within the bound.
A program may use at most 64 MiB of HBM per device.

v0:
```python
import jax
import jax.numpy as jnp
from jax import lax
from jax.sharding import PartitionSpec as P

epsilon = 1e-05


def normalize(values, channel_dim):
    values = values.astype(jnp.float32)
    centred = values - jnp.mean(values, axis=channel_dim, keepdims=True)
    spread = jnp.mean(centred * centred, axis=channel_dim, keepdims=True)
    return centred / jnp.sqrt(spread + epsilon)


def triangle_product(exchanged, n_row, n_col):
    left_part = exchanged[0]
    right_part = exchanged[1]
    item_count = left_part.shape[2]
    tok_row = left_part.shape[3]
    tok_col = left_part.shape[4]
    product = jnp.einsum(
        "ruxiq,suxjq->xrisj", left_part, right_part, preferred_element_type=jnp.float32
    )
    product = product.reshape(item_count, n_row, tok_row, n_col, tok_col)
    return product.transpose(1, 3, 0, 2, 4).astype(jnp.bfloat16)


def on_device(
    pair_grid,
    alignment_pool,
    sample_index,
    token_mask,
    outer_proj,
    outer_mix,
    pair_logit,
    average_proj,
    average_mix,
    triangle_proj,
    triangle_mix,
    transition_up,
    transition_down,
):
    n_row = lax.axis_size("row")
    n_col = lax.axis_size("col")
    tok_row = pair_grid.shape[0]
    tok_col = pair_grid.shape[1]
    pair_width = pair_grid.shape[2]
    samples = sample_index.shape[0]
    align_width = alignment_pool.shape[2]
    outer_width = outer_proj.shape[1] // 2
    head_count = pair_logit.shape[1]
    head_total = average_proj.shape[1] // 2
    head_dim = head_total // head_count
    inner_width = transition_down.shape[0]
    row_start = lax.axis_index("row") * tok_row
    column_start = lax.axis_index("col") * tok_col
    alignments = jnp.take(alignment_pool, sample_index, axis=0)
    align_norm = normalize(alignments, 2).astype(jnp.bfloat16)
    align_rows = align_norm.reshape(samples, tok_row * align_width)
    gathered = lax.all_gather(align_rows, "row", axis=1, tiled=True)
    column_flat = lax.dynamic_slice_in_dim(
        gathered, column_start * align_width, tok_col * align_width, 1
    )
    column_norm = column_flat.reshape(samples, tok_col, align_width)
    row_factor = jnp.dot(
        align_norm, outer_proj[:, :outer_width], preferred_element_type=jnp.float32
    ).astype(jnp.bfloat16)
    column_factor = jnp.dot(
        column_norm, outer_proj[:, outer_width:], preferred_element_type=jnp.float32
    ).astype(jnp.bfloat16)
    column_rows = column_factor.reshape(samples, tok_col * outer_width)
    block_rows = 8
    block_count = tok_row // block_rows
    row_blocks = row_factor.reshape(samples, block_count, block_rows * outer_width).transpose(
        1, 0, 2
    )
    pair_blocks = pair_grid.reshape(block_count, block_rows, tok_col, pair_width)

    def outer_step(operands):
        left_block, pair_block = operands
        outer_sum = lax.dot_general(
            left_block, column_rows, (((0,), (0,)), ((), ())), preferred_element_type=jnp.float32
        )
        outer_sum = outer_sum.reshape(block_rows, outer_width, tok_col, outer_width).transpose(
            0, 2, 1, 3
        )
        outer_mean = (
            (outer_sum * (1.0 / samples))
            .astype(jnp.bfloat16)
            .reshape(block_rows * tok_col, outer_width * outer_width)
        )
        update = jnp.dot(outer_mean, outer_mix, preferred_element_type=jnp.float32).reshape(
            block_rows, tok_col, pair_width
        )
        return (pair_block.astype(jnp.float32) + update).astype(jnp.bfloat16)

    pair_one = lax.map(outer_step, (row_blocks, pair_blocks)).reshape(tok_row, tok_col, pair_width)
    pair_norm = normalize(pair_one, 2).astype(jnp.bfloat16)
    value_weight = average_proj[:, :head_total].reshape(align_width, head_count, head_dim)
    gate_weight = average_proj[:, head_total:].reshape(align_width, head_count, head_dim)
    mix_weight = average_mix.reshape(head_count, head_dim, align_width)
    scores = lax.dot_general(
        pair_logit, pair_norm, (((0,), (2,)), ((), ())), preferred_element_type=jnp.float32
    )
    weights = jnp.exp(scores)
    partial_total = jnp.sum(weights, axis=2)
    weights_low = weights.astype(jnp.bfloat16)
    column_values = jnp.einsum(
        "sjm,mhc->hjsc", column_norm, value_weight, preferred_element_type=jnp.float32
    )
    column_values = column_values.astype(jnp.bfloat16).reshape(
        head_count, tok_col, samples * head_dim
    )
    partial_sum = jnp.einsum(
        "hij,hjk->hik", weights_low, column_values, preferred_element_type=jnp.float32
    )
    weighted, totals = (
        lax.psum(partial_sum.astype(jnp.bfloat16), "col").astype(jnp.float32),
        lax.psum(partial_total.astype(jnp.bfloat16), "col").astype(jnp.float32),
    )
    gate_values = jax.nn.sigmoid(
        jnp.einsum("sim,mhc->hisc", align_norm, gate_weight, preferred_element_type=jnp.float32)
    )
    weighted = weighted.reshape(head_count, tok_row, samples, head_dim)
    averaged = (gate_values * weighted / totals[:, :, None, None]).astype(jnp.bfloat16)
    align_update = jnp.einsum(
        "hisc,hcm->sim", averaged, mix_weight, preferred_element_type=jnp.float32
    )
    alignment_next = (alignments.astype(jnp.float32) + align_update).astype(jnp.bfloat16)
    flat_norm = pair_norm.reshape(tok_row * tok_col, pair_width)
    projected = lax.dot_general(
        triangle_proj[:, : 4 * pair_width],
        flat_norm,
        (((0,), (1,)), ((), ())),
        preferred_element_type=jnp.float32,
    )
    projected = projected.reshape(4, pair_width, tok_row, tok_col)
    row_mask = lax.dynamic_slice_in_dim(token_mask, row_start, tok_row, 0).astype(jnp.float32)
    column_mask = lax.dynamic_slice_in_dim(token_mask, column_start, tok_col, 0).astype(jnp.float32)
    pair_mask = row_mask[:, None] * column_mask[None, :]
    left_side = jax.nn.sigmoid(projected[0]) * projected[1] * pair_mask
    right_side = jax.nn.sigmoid(projected[2]) * projected[3] * pair_mask
    factors = jnp.stack([left_side, right_side]).astype(jnp.bfloat16)
    group_size = pair_width // (n_row * n_col)
    grouped = factors.reshape(2, n_row * n_col, group_size, tok_row, tok_col)
    received = lax.all_to_all(grouped, ("row", "col"), split_axis=1, concat_axis=1, tiled=True)
    arranged = received.reshape(2, n_row, n_col, received.shape[2], tok_row, tok_col)
    result = triangle_product(arranged, n_row, n_col)
    flat_result = result.reshape(n_row * n_col, result.shape[2], tok_row, tok_col)
    product = lax.all_to_all(flat_result, ("row", "col"), split_axis=0, concat_axis=0, tiled=True)
    product = product.reshape(pair_width, tok_row, tok_col)
    product_norm = normalize(product, 0).astype(jnp.bfloat16).reshape(pair_width, tok_row * tok_col)
    mixed = lax.dot_general(
        product_norm, triangle_mix, (((0,), (0,)), ((), ())), preferred_element_type=jnp.float32
    )
    gate_out = jax.nn.sigmoid(
        jnp.dot(flat_norm, triangle_proj[:, 4 * pair_width :], preferred_element_type=jnp.float32)
    )
    pair_two = (
        pair_one.reshape(tok_row * tok_col, pair_width).astype(jnp.float32) + gate_out * mixed
    ).astype(jnp.bfloat16)
    tail_rows = pair_two.reshape(block_count, block_rows * tok_col, pair_width)

    def transition_step(rows_block):
        normed = normalize(rows_block, 1).astype(jnp.bfloat16)
        expanded = jnp.dot(normed, transition_up, preferred_element_type=jnp.float32)
        hidden = (jax.nn.silu(expanded[:, :inner_width]) * expanded[:, inner_width:]).astype(
            jnp.bfloat16
        )
        return (
            rows_block.astype(jnp.float32)
            + jnp.dot(hidden, transition_down, preferred_element_type=jnp.float32)
        ).astype(jnp.bfloat16)

    pair_next = lax.map(transition_step, tail_rows).reshape(tok_row, tok_col, pair_width)
    return (pair_next, alignment_next)


def solution(mesh):
    in_specs = (
        P(("groups", "row"), "col", None),
        P("groups", "row", None),
        P("groups"),
        P("groups"),
        P(),
        P(),
        P(),
        P(),
        P(),
        P(),
        P(),
        P(),
        P(),
    )
    out_specs = (P(("groups", "row"), "col", None), P("groups", "row", None))
    return jax.shard_map(
        on_device, mesh=mesh, in_specs=in_specs, out_specs=out_specs, check_vma=False
    )
```

profile of v0, /device:TPU:0, one launch (start us, length us, event | category | flops | bytes accessed | tf_op | source)
XLA Modules:
  0.0 163.6 jit_solution(2614358065298384016)
XLA Ops:
  8.5 2.0 %copy.82 = bf16[256,16,64]{2,1,0:T(8,128)(2,1)S(1)} copy(bf16[256,16,64]{0,2,1:T(8,128)(2,1)} %param.18) | data formatting | bytes 1048576 | tf_op args[1]
  14.1 1.2 convolution_convert_fusion.2
  15.3 42.9 %all-gather.2.cloned.1.call-done = bf16[64,16384]{1,0:T(8,128)(2,1)} async-done(((bf16[64,1024]{1,0:T(8,128)(2,1)}), bf16[64,16384]{1,0:T(8,128)(2,1)}) %all-gather.2.cloned.1.call-update) | async-done | bytes 2097168 | tf_op jit(solution)/shard_map/all_gather | solution.py:61
  58.2 2.3 %constant_dynamic-slice_fusion.1 = bf16[64,8192]{1,0:T(8,128)(2,1)} fusion(bf16[64,16384]{1,0:T(8,128)(2,1)} %all-gather.2.cloned.1.call-done, s32[]{:T(128)S(6)} %select_n.24), kind=kLoop, calls=%fused_computation.116 | loop fusion | bytes 2097156 | tf_op jit(solution)/shard_map/dynamic_slice | solution.py:62
  60.5 3.3 %reshape.294 = bf16[64,128,64]{2,1,0:T(8,128)(2,1)S(1)} reshape(bf16[64,8192]{1,0:T(8,128)(2,1)} %constant_dynamic-slice_fusion.1) | data formatting | bytes 2097152 | tf_op jit(solution)/shard_map/reshape | solution.py:65
  63.8 1.3 copy-done.1
  65.1 0.9 convolution_convert_fusion.1
  66.0 1.7 %copy.89 = bf16[64,128,32]{0,2,1:T(8,128)(2,1)S(1)} copy(bf16[64,128,32]{1,2,0:T(8,128)(2,1)S(1)} %convolution_convert_fusion.1) | data formatting | bytes 1048576 | tf_op jit(solution)/shard_map/convert_element_type | solution.py:71
  67.7 9.3 %while.20 = (s32[]{:T(128)}, bf16[2,8,128,128]{3,2,1,0:T(8,128)(2,1)S(1)}, bf16[2,8,128,128]{3,2,1,0:T(8,128)(2,1)}, bf16[2,64,256]{1,2,0:T(8,128)(2,1)}, bf16[6...) while((s32[]{:T(128)}, bf16[2,8,128,128]{3,2,1,0:T(8,128)(2,1)S(1)}, ...), condition=%wide.region_3.4_spmd, body=%wide.region_2.3_spmd.sunk | while | flops 405143552 | bytes 13992077 | solution.py:98
  68.6 1.1 copy.148
  73.2 1.1 copy.148
  80.0 1.6 slice_multiply_fusion.2
  82.1 1.6 copy.91
  84.2 1.2 copy.92
  85.5 3.5 %all-to-all-start = ((bf16[2,32,4,16,128]{4,3,2,0,1:T(8,128)(2,1)}), bf16[2,32,4,16,128]{4,3,2,0,1:T(8,128)(2,1)}, u32[]{:S(2)}, u32[]{:S(2)}) async-start(bf16[2,32,4,16,128]{4,3,2,0,1:T(8,128)(2,1)} %copy.92), calls=%async_computation | async-start | bytes 2097152 | tf_op jit(solution)/shard_map/all_to_all | solution.py:147
  89.4 1.3 convert_bitcast_fusion.1
  92.5 1.2 convolution_convert_fusion
  93.7 1.6 %reshape.302 = bf16[8,16,64,32]{3,2,1,0:T(8,128)(2,1)S(1)} reshape(bf16[8,16,2048]{2,1,0:T(8,128)(2,1)S(1)} %convolution_convert_fusion) | data formatting | bytes 1048576 | tf_op jit(solution)/shard_map/reshape | solution.py:125
  95.3 1.6 copy.103
  97.0 18.1 %all-to-all-done = bf16[2,32,4,16,128]{4,3,2,0,1:T(8,128)(2,1)} async-done(((bf16[2,32,4,16,128]{4,3,2,0,1:T(8,128)(2,1)}), bf16[2,32,4,16,128]{4,3,2,0,1:T(8,128)(2,1)}, u32[]{:S(2)}, u32[]{:S(2)}) %all-to-all-start) | async-done | bytes 1048608 | tf_op jit(solution)/shard_map/all_to_all | solution.py:147
  115.1 1.4 fusion.76
  116.6 1.3 bitcast_convert_fusion
  117.9 3.0 %copy.95 = bf16[4,16,16,16,16]{4,3,2,1,0:T(8,128)(2,1)} copy(bf16[4,16,16,16,16]{4,2,3,1,0:T(8,128)(2,1)S(1)} %bitcast_convert_fusion) | data formatting | bytes 1048576 | tf_op jit(solution)/shard_map/convert_element_type | solution.py:26
  120.9 5.8 %convert_element_type.146 = bf16[4,16,16,2,128]{4,3,2,1,0:T(2,128)(2,1)S(1)} reshape(bf16[4,16,16,16,16]{4,3,2,1,0:T(8,128)(2,1)} %copy.95) | data formatting | bytes 1048576 | tf_op jit(solution)/shard_map/convert_element_type | solution.py:26
  126.7 0.9 copy.96
  127.7 3.6 %all-to-all-start.1 = ((bf16[32,4,16,128]{3,2,1,0:T(8,128)(2,1)}), bf16[32,4,16,128]{3,2,1,0:T(8,128)(2,1)S(1)}, u32[]{:S(2)}, u32[]{:S(2)}) async-start(bf16[32,4,16,128]{3,2,1,0:T(8,128)(2,1)} %bitcast.34), calls=%async_computation.1 | async-start | bytes 1048576 | tf_op jit(solution)/shard_map/all_to_all | solution.py:151
  131.6 8.5 %psum.15 = bf16[8,16]{1,0:T(8,128)(2,1)S(1)} all-reduce(bf16[8,16]{1,0:T(8,128)(2,1)S(1)} %copy.104), channel_id=1, replica_groups=mesh['groups'=1,'row'=16,'col'=2] {'col'}, use_global_device_ids=true, to_apply=%region_14.15 | all-reduce | flops 128 | bytes 512 | tf_op jit(solution)/shard_map/psum | solution.py:120
  140.2 2.1 %fusion.26 = f32[2048,128]{1,0:T(8,128)} fusion(bf16[2048,128]{1,0:T(8,128)(2,1)S(1)} %copy-done.5, bf16[128,640]{1,0:T(8,128)(2,1)} %param.26), kind=kOutput, calls=%fused_computation.39 | convolution fusion | flops 67895296 | bytes 1605632 | tf_op jit(solution)/shard_map/dot_general | solution.py:158
  142.3 3.7 %all-reduce.2.cloned.1.call-done = bf16[8,16,64,32]{2,3,1,0:T(8,128)(2,1)} async-done(((bf16[8,16,64,32]{2,3,1,0:T(8,128)(2,1)}), bf16[8,16,64,32]{2,3,1,0:T(8,128)(2,1)}) %all-reduce.2.cloned.1.call-update) | async-done | bytes 524304 | tf_op jit(solution)/shard_map/psum | solution.py:119
  146.1 2.5 %fusion.32 = bf16[64,16,64]{2,0,1:T(8,128)(2,1)S(1)} fusion(bf16[8,32,64,1]{2,1,3,0:T(8,128)(2,1)S(1)} %bitcast.239, bf16[8,16,64,32]{2,3,1,0:T(8,128)(2,1)} %all-reduce.2.cloned.1.call-done, bf16[64,8,32,1]{0,2,3,1:T(8,128)(2,1)S(1)} %bitcast.238, f32[8,16]{1,0:T(8,128)S(1)} %convert_element_type.161, f32[64,16]{0,1:T(8,128)S(1)} %add_sqrt_fusion.2, ...), kind=kOutput, calls=%fused_computation.49 | convolution fusion | flops 69533696 | bytes 860736 | tf_op jit(solution)/shard_map/hisc,hcm->sim/dot_general | solution.py:127
  149.9 1.8 %fusion.27 = bf16[2048,128]{1,0:T(8,128)(2,1)S(1)} fusion(f32[2048,128]{1,0:T(8,128)} %fusion.26, bf16[128,128]{1,0:T(8,128)(2,1)S(1)} %copy-done, f32[16,8,16,128]{3,2,1,0:T(8,128)S(1)} %bitcast_convert_fusion.1, f32[2048]{0:T(1024)S(1)} %sqrt_bitcast_fusion, f32[2048]{0:T(1024)S(1)} %get-tuple-element.106, bf16[2048,128]{1,0:T(8,128)(2,1)S(1)} %bitcast.227), kind=kOutput, calls=%fused_computation.41 | convolution fusion | flops 68943872 | bytes 3194880 | tf_op jit(solution)/shard_map/dot_general | solution.py:154
  151.8 4.2 %while.21 = (s32[]{:T(128)}, bf16[2,1024,128]{2,1,0:T(8,128)(2,1)S(1)}, bf16[2,1024,128]{2,1,0:T(8,128)(2,1)S(1)}, bf16[128,1024]{1,0:T(8,128)(2,1)S(1)}, bf16[512,128]{1,0:T(8,128)(2,1)S(1)}, /*index=5*/s32[]{:T(128)}) while((s32[]{:T(128)}, bf16[2,1024,128]{2,1,0:T(8,128)(2,1)S(1)}, bf16[2,1024,128]{2,1,0:T(8,128)(2,1)S(1)}, ...), condition=%wide.region_11.12_spmd, body=%wide.region_8.11_spmd.sunk | while | flops 407503872 | bytes 10129493 | solution.py:176
  (109 shorter events, 24.8 us)
Async XLA Ops:
  7.2 142.7 %copy-start = (bf16[128,128]{1,0:T(8,128)(2,1)S(1)}, bf16[128,128]{1,0:T(8,128)(2,1)}, u32[]{:S(2)}) copy-start(bf16[128,128]{1,0:T(8,128)(2,1)} %param.27) | copy-start | bytes 98308
  7.2 51.0 %all-gather.2.cloned.1.call-start = ((), (), s32[]{:S(2)}) async-start(), calls=%async_computation.2 | async-start | bytes 2228224 | tf_op jit(solution)/shard_map/all_gather | solution.py:61
  11.9 2.0 %copy-start.14 = (s32[256]{0:T(256)S(1)}, s32[256]{0:T(256)}, u32[]{:S(2)}) copy-start(s32[256]{0:T(256)} %param.20) | copy-start | bytes 3076
  11.9 2.2 %copy-start.9 = (bf16[64,64]{1,0:T(8,128)(2,1)S(1)}, bf16[64,64]{1,0:T(8,128)(2,1)}, u32[]{:S(2)}) copy-start(bf16[64,64]{1,0:T(8,128)(2,1)} %param.21) | copy-start | bytes 24580
  63.8 1.3 copy-start.1
  70.4 1.0 copy-start.11
  70.4 1.1 copy-start.12
  75.0 1.0 copy-start.11
  75.0 1.1 copy-start.12
  77.0 2.3 %copy-start.6 = (bf16[128,640]{1,0:T(8,128)(2,1)S(1)}, bf16[128,640]{1,0:T(8,128)(2,1)}, u32[]{:S(2)}) copy-start(bf16[128,640]{1,0:T(8,128)(2,1)} %param.26) | copy-start | bytes 491524
  78.5 0.8 copy-start.4
  84.2 5.0 %copy-start.7 = (bf16[64,512]{1,0:T(8,128)(2,1)S(1)}, bf16[64,512]{1,0:T(8,128)(2,1)}, u32[]{:S(2)}) copy-start(bf16[64,512]{1,0:T(8,128)(2,1)} %param.24) | copy-start | bytes 196612
  84.2 5.1 %copy-start.2 = (bf16[64,128,64]{2,1,0:T(8,128)(2,1)S(1)}, bf16[64,128,64]{2,1,0:T(8,128)(2,1)}, u32[]{:S(2)}) copy-start(bf16[64,128,64]{2,1,0:T(8,128)(2,1)} %copy-done.1) | copy-start | bytes 3145732
  85.5 29.6 %all-to-all-start = ((bf16[2,32,4,16,128]{4,3,2,0,1:T(8,128)(2,1)}), bf16[2,32,4,16,128]{4,3,2,0,1:T(8,128)(2,1)}, u32[]{:S(2)}, u32[]{:S(2)}) async-start(bf16[2,32,4,16,128]{4,3,2,0,1:T(8,128)(2,1)} %copy.92), calls=%async_computation | async-start | bytes 2097152 | tf_op jit(solution)/shard_map/all_to_all | solution.py:147
  88.9 57.1 %all-reduce.2.cloned.1.call-start = ((), (), s32[]{:S(2)}) async-start(), calls=%async_computation.3 | async-start | bytes 2097152 | tf_op jit(solution)/shard_map/psum | solution.py:119
  90.6 1.5 copy-start.10
  126.7 4.7 %copy-start.8 = (bf16[256,64]{0,1:T(8,128)(2,1)S(1)}, bf16[256,64]{0,1:T(8,128)(2,1)}, u32[]{:S(2)}) copy-start(bf16[256,64]{0,1:T(8,128)(2,1)} %param.25) | copy-start | bytes 98308
  126.7 13.5 %copy-start.5 = (bf16[2048,128]{1,0:T(8,128)(2,1)S(1)}, bf16[2048,128]{1,0:T(8,128)(2,1)}, u32[]{:S(2)}) copy-start(bf16[2048,128]{1,0:T(8,128)(2,1)} %copy-done.4) | copy-start | bytes 1572868
  127.7 21.7 %all-to-all-start.1 = ((bf16[32,4,16,128]{3,2,1,0:T(8,128)(2,1)}), bf16[32,4,16,128]{3,2,1,0:T(8,128)(2,1)S(1)}, u32[]{:S(2)}, u32[]{:S(2)}) async-start(bf16[32,4,16,128]{3,2,1,0:T(8,128)(2,1)} %bitcast.34), calls=%async_computation.1 | async-start | bytes 1048576 | tf_op jit(solution)/shard_map/all_to_all | solution.py:151
  149.9 1.8 %copy-start.3 = (bf16[128,1024]{1,0:T(8,128)(2,1)S(1)}, bf16[128,1024]{1,0:T(8,128)(2,1)}, u32[]{:S(2)}) copy-start(bf16[128,1024]{1,0:T(8,128)(2,1)} %param.28) | copy-start | bytes 786436
  149.9 1.8 %copy-start.13 = (bf16[512,128]{1,0:T(8,128)(2,1)S(1)}, bf16[512,128]{1,0:T(8,128)(2,1)}, u32[]{:S(2)}) copy-start(bf16[512,128]{1,0:T(8,128)(2,1)} %param.29) | copy-start | bytes 393220
  156.0 0.8 copy-start.15
Sparse Core Ops, SparseCore 0:
  14.0 44.1 all-gather.1
  97.1 48.9 all-reduce.1
where the time goes:
time: 165 us; the launch traced here: 164 us
  waiting for transfers between devices  64.8 us (39%)
  local copies, waits for them, and re-layouts  40.2 us (24%)
  matrix products  19.4 us (12%)
  between operations  14.5 us (9%)
  blocking collectives  8.55 us (5%)
  other arithmetic  8.53 us (5%)
  starting transfers between devices  7.4 us (4%)
    all_gather x1, waiting for transfers between devices, on_device(): gathered = lax.all_gather(align_rows, 'row', axis=1, tiled=True)  42.9 us
    all_to_all x1, waiting for transfers between devices, on_device(): lax.all_to_all(grouped, ('row', 'col'), split_axis=1, concat_axis=1, tile...  18.1 us
    convert_element_type x3, local copies, waits for them, and re-layouts, triangle_product(): return product.transpose(1, 3, 0, 2, 4).astype(jnp.bfloat16)  9.76 us
    psum x1, blocking collectives, on_device(): lax.psum(partial_total.astype(jnp.bfloat16), 'col').astype(jnp.float32)  8.55 us
    unnamed x36, local copies, waits for them, and re-layouts  6.61 us
    psum x1, waiting for transfers between devices, on_device(): lax.psum(partial_sum.astype(jnp.bfloat16), 'col').astype(jnp.float32)  3.71 us
    all_to_all x1, starting transfers between devices, on_device(): lax.all_to_all(flat_result, ('row', 'col'), split_axis=0, concat_axis=0,...  3.64 us
    all_to_all x1, starting transfers between devices, on_device(): lax.all_to_all(grouped, ('row', 'col'), split_axis=1, concat_axis=1, tile...  3.46 us
  transfers between devices with their start and end apart: 4, of which 3 were waited for; matrix products, arithmetic and copies ran while one was open for 17% of the time, Pallas kernels for 0%

commit v1 on v0

--- a/solution.py
+++ b/solution.py
@@ -144,7 +144,9 @@
     factors = jnp.stack([left_side, right_side]).astype(jnp.bfloat16)
     group_size = pair_width // (n_row * n_col)
     grouped = factors.reshape(2, n_row * n_col, group_size, tok_row, tok_col)
-    received = lax.all_to_all(grouped, ("row", "col"), split_axis=1, concat_axis=1, tiled=True)
+    y2 = lax.axis_size(("row", "col"))
+    response = jnp.stack(jnp.split(grouped, y2, 1), 0)
+    received = jnp.concatenate(lax.all_to_all(response, ("row", "col"), 0, 0), 1)
     arranged = received.reshape(2, n_row, n_col, received.shape[2], tok_row, tok_col)
     result = triangle_product(arranged, n_row, n_col)
     flat_result = result.reshape(n_row * n_col, result.shape[2], tok_row, tok_col)

time: 165 us -> 183 us (1.11)
  other arithmetic: 8.53 us -> 27.8 us
    unnamed x1 -> x32, other arithmetic: 0.11 us -> 18.8 us
  transfers between devices with their start and end apart: 4 -> 4, of which waited for: 3 -> 3; matrix products, arithmetic and copies ran while one was open for 17% -> 15% of each run, Pallas kernels for 0% -> 0%
where the time goes in v1:
time: 183 us; the launch traced here: 182 us
  waiting for transfers between devices  64.8 us (35%)
  local copies, waits for them, and re-layouts  39 us (21%)
  other arithmetic  27.8 us (15%)
  matrix products  19.5 us (11%)
  between operations  14.5 us (8%)
  blocking collectives  8.54 us (5%)
  starting transfers between devices  7.39 us (4%)
    all_gather x1, waiting for transfers between devices, on_device(): gathered = lax.all_gather(align_rows, 'row', axis=1, tiled=True)  42.9 us
    unnamed x32, other arithmetic  18.8 us
    all_to_all x1, waiting for transfers between devices, on_device(): lax.all_to_all(response, ('row', 'col'), 0, 0)  18.1 us
    convert_element_type x3, local copies, waits for them, and re-layouts, triangle_product(): return product.transpose(1, 3, 0, 2, 4).astype(jnp.bfloat16)  9.76 us
    psum x1, blocking collectives, on_device(): lax.psum(partial_total.astype(jnp.bfloat16), 'col').astype(jnp.float32)  8.54 us
    unnamed x36, local copies, waits for them, and re-layouts  6.6 us
    psum x1, waiting for transfers between devices, on_device(): lax.psum(partial_sum.astype(jnp.bfloat16), 'col').astype(jnp.float32)  3.71 us
  transfers between devices with their start and end apart: 4, of which 3 were waited for; matrix products, arithmetic and copies ran while one was open for 15% of the time, Pallas kernels for 0%

profile of v1, /device:TPU:0, one launch (start us, length us, event | category | flops | bytes accessed | tf_op | source)
XLA Modules:
  0.0 181.6 jit_solution(9011661152855975141)
XLA Ops:
  8.5 2.0 %copy.172 = bf16[256,16,64]{2,1,0:T(8,128)(2,1)S(1)} copy(bf16[256,16,64]{0,2,1:T(8,128)(2,1)} %param.18) | data formatting | bytes 1048576 | tf_op args[1]
  14.1 1.2 convolution_convert_fusion.2
  15.3 42.9 %all-gather.2.cloned.1.call-done = bf16[64,16384]{1,0:T(8,128)(2,1)} async-done(((bf16[64,1024]{1,0:T(8,128)(2,1)}), bf16[64,16384]{1,0:T(8,128)(2,1)}) %all-gather.2.cloned.1.call-update) | async-done | bytes 2097168 | tf_op jit(solution)/shard_map/all_gather | solution.py:61
  58.2 2.3 %constant_dynamic-slice_fusion.1 = bf16[64,8192]{1,0:T(8,128)(2,1)} fusion(bf16[64,16384]{1,0:T(8,128)(2,1)} %all-gather.2.cloned.1.call-done, s32[]{:T(128)S(6)} %select_n.24), kind=kLoop, calls=%fused_computation.242 | loop fusion | bytes 2097156 | tf_op jit(solution)/shard_map/dynamic_slice | solution.py:62
  60.5 3.3 %reshape.296 = bf16[64,128,64]{2,1,0:T(8,128)(2,1)S(1)} reshape(bf16[64,8192]{1,0:T(8,128)(2,1)} %constant_dynamic-slice_fusion.1) | data formatting | bytes 2097152 | tf_op jit(solution)/shard_map/reshape | solution.py:65
  63.8 1.3 copy-done.1
  65.1 0.9 convolution_convert_fusion.1
  66.0 1.7 copy.179
  67.7 9.3 %while.20 = (s32[]{:T(128)}, bf16[2,8,128,128]{3,2,1,0:T(8,128)(2,1)S(1)}, bf16[2,8,128,128]{3,2,1,0:T(8,128)(2,1)}, bf16[2,64,256]{1,2,0:T(8,128)(2,1)}, bf16[6...) while((s32[]{:T(128)}, bf16[2,8,128,128]{3,2,1,0:T(8,128)(2,1)S(1)}, ...), condition=%wide.region_3.4_spmd, body=%wide.region_2.3_spmd.sunk | while | flops 405143552 | bytes 13992077 | solution.py:98
  68.6 1.1 copy.297
  73.2 1.1 copy.297
  80.0 1.6 slice_multiply_fusion.2
  82.1 1.6 copy.181
  103.5 3.4 %all-to-all-start = ((bf16[32,2,1,4,16,128]{5,4,3,1,2,0:T(8,128)(2,1)}), bf16[32,2,1,4,16,128]{5,4,3,1,2,0:T(8,128)(2,1)}, u32[]{:S(2)}, u32[]{:S(2)}) async-start(bf16[32,2,1,4,16,128]{5,4,3,1,2,0:T(8,128)(2,1)} %constant_dynamic-update-slice_fusion), calls=%async_computation | async-start | bytes 2097152 | tf_op jit(solution)/shard_map/all_to_all | solution.py:149
  107.3 1.3 convert_bitcast_fusion.1
  108.6 0.9 copy.219
  110.5 1.2 convolution_convert_fusion
  111.7 1.6 reshape.305
  113.3 1.6 copy.222
  115.0 18.1 %all-to-all-done = bf16[32,2,1,4,16,128]{5,4,3,1,2,0:T(8,128)(2,1)} async-done(((bf16[32,2,1,4,16,128]{5,4,3,1,2,0:T(8,128)(2,1)}), bf16[32,2,1,4,16,128]{5,4,3,1,2,0:T(8,128)(2,1)}, u32[]{:S(2)}, u32[]{:S(2)}) %all-to-all-start) | async-done | bytes 1048608 | tf_op jit(solution)/shard_map/all_to_all | solution.py:149
  133.1 1.4 fusion.108
  134.6 1.3 bitcast_convert_fusion
  135.9 3.0 %copy.214 = bf16[4,16,16,16,16]{4,3,2,1,0:T(8,128)(2,1)} copy(bf16[4,16,16,16,16]{4,2,3,1,0:T(8,128)(2,1)S(1)} %bitcast_convert_fusion) | data formatting | bytes 1048576 | tf_op jit(solution)/shard_map/convert_element_type | solution.py:26
  138.9 5.8 %convert_element_type.146 = bf16[4,16,16,2,128]{4,3,2,1,0:T(2,128)(2,1)S(1)} reshape(bf16[4,16,16,16,16]{4,3,2,1,0:T(8,128)(2,1)} %copy.214) | data formatting | bytes 1048576 | tf_op jit(solution)/shard_map/convert_element_type | solution.py:26
  144.7 0.9 copy.215
  145.6 3.6 %all-to-all-start.1 = ((bf16[32,4,16,128]{3,2,1,0:T(8,128)(2,1)}), bf16[32,4,16,128]{3,2,1,0:T(8,128)(2,1)S(1)}, u32[]{:S(2)}, u32[]{:S(2)}) async-start(bf16[32,4,16,128]{3,2,1,0:T(8,128)(2,1)} %bitcast.67), calls=%async_computation.1 | async-start | bytes 1048576 | tf_op jit(solution)/shard_map/all_to_all | solution.py:153
  149.6 8.5 %psum.15 = bf16[8,16]{1,0:T(8,128)(2,1)S(1)} all-reduce(bf16[8,16]{1,0:T(8,128)(2,1)S(1)} %copy.223), channel_id=1, replica_groups=mesh['groups'=1,'row'=16,'col'=2] {'col'}, use_global_device_ids=true, to_apply=%region_14.15 | all-reduce | flops 128 | bytes 512 | tf_op jit(solution)/shard_map/psum | solution.py:120
  158.2 2.2 %fusion.26 = f32[2048,128]{1,0:T(8,128)} fusion(bf16[2048,128]{1,0:T(8,128)(2,1)S(1)} %copy-done.5, bf16[128,640]{1,0:T(8,128)(2,1)} %param.26), kind=kOutput, calls=%fused_computation.101 | convolution fusion | flops 67895296 | bytes 1605632 | tf_op jit(solution)/shard_map/dot_general | solution.py:160
  160.3 3.7 %all-reduce.2.cloned.1.call-done = bf16[8,16,64,32]{2,3,1,0:T(8,128)(2,1)} async-done(((bf16[8,16,64,32]{2,3,1,0:T(8,128)(2,1)}), bf16[8,16,64,32]{2,3,1,0:T(8,128)(2,1)}) %all-reduce.2.cloned.1.call-update) | async-done | bytes 524304 | tf_op jit(solution)/shard_map/psum | solution.py:119
  164.0 2.5 %fusion.32 = bf16[64,16,64]{2,0,1:T(8,128)(2,1)S(1)} fusion(bf16[8,32,64,1]{2,1,3,0:T(8,128)(2,1)S(1)} %bitcast.366, bf16[8,16,64,32]{2,3,1,0:T(8,128)(2,1)} %all-reduce.2.cloned.1.call-done, bf16[64,8,32,1]{0,2,3,1:T(8,128)(2,1)S(1)} %bitcast.365, f32[8,16]{1,0:T(8,128)S(1)} %convert_element_type.161, f32[64,16]{0,1:T(8,128)S(1)} %add_sqrt_fusion.2, ...), kind=kOutput, calls=%fused_computation.111 | convolution fusion | flops 69533696 | bytes 860736 | tf_op jit(solution)/shard_map/hisc,hcm->sim/dot_general | solution.py:127
  167.9 1.8 fusion.27
  169.8 4.2 %while.21 = (s32[]{:T(128)}, bf16[2,1024,128]{2,1,0:T(8,128)(2,1)S(1)}, bf16[2,1024,128]{2,1,0:T(8,128)(2,1)S(1)}, bf16[128,1024]{1,0:T(8,128)(2,1)S(1)}, bf16[512,128]{1,0:T(8,128)(2,1)S(1)}, /*index=5*/s32[]{:T(128)}) while((s32[]{:T(128)}, bf16[2,1024,128]{2,1,0:T(8,128)(2,1)S(1)}, bf16[2,1024,128]{2,1,0:T(8,128)(2,1)S(1)}, ...), condition=%wide.region_11.12_spmd, body=%wide.region_8.11_spmd.sunk | while | flops 407503872 | bytes 10129493 | solution.py:178
  (139 shorter events, 43.1 us)
Async XLA Ops:
  7.2 160.7 %copy-start = (bf16[128,128]{1,0:T(8,128)(2,1)S(1)}, bf16[128,128]{1,0:T(8,128)(2,1)}, u32[]{:S(2)}) copy-start(bf16[128,128]{1,0:T(8,128)(2,1)} %param.27) | copy-start | bytes 98308
  7.2 51.0 %all-gather.2.cloned.1.call-start = ((), (), s32[]{:S(2)}) async-start(), calls=%async_computation.2 | async-start | bytes 2228224 | tf_op jit(solution)/shard_map/all_gather | solution.py:61
  11.9 2.0 %copy-start.14 = (s32[256]{0:T(256)S(1)}, s32[256]{0:T(256)}, u32[]{:S(2)}) copy-start(s32[256]{0:T(256)} %param.20) | copy-start | bytes 3076
  11.9 2.2 %copy-start.9 = (bf16[64,64]{1,0:T(8,128)(2,1)S(1)}, bf16[64,64]{1,0:T(8,128)(2,1)}, u32[]{:S(2)}) copy-start(bf16[64,64]{1,0:T(8,128)(2,1)} %param.21) | copy-start | bytes 24580
  63.8 1.3 copy-start.1
  70.4 1.0 copy-start.11
  70.4 1.1 copy-start.12
  75.0 1.0 copy-start.11
  75.0 1.1 copy-start.12
  77.0 2.3 %copy-start.6 = (bf16[128,640]{1,0:T(8,128)(2,1)S(1)}, bf16[128,640]{1,0:T(8,128)(2,1)}, u32[]{:S(2)}) copy-start(bf16[128,640]{1,0:T(8,128)(2,1)} %param.26) | copy-start | bytes 491524
  78.5 0.8 copy-start.4
  102.2 5.0 %copy-start.7 = (bf16[64,512]{1,0:T(8,128)(2,1)S(1)}, bf16[64,512]{1,0:T(8,128)(2,1)}, u32[]{:S(2)}) copy-start(bf16[64,512]{1,0:T(8,128)(2,1)} %param.24) | copy-start | bytes 196612
  102.2 5.1 %copy-start.2 = (bf16[64,128,64]{2,1,0:T(8,128)(2,1)S(1)}, bf16[64,128,64]{2,1,0:T(8,128)(2,1)}, u32[]{:S(2)}) copy-start(bf16[64,128,64]{2,1,0:T(8,128)(2,1)} %copy-done.1) | copy-start | bytes 3145732
  103.5 29.6 %all-to-all-start = ((bf16[32,2,1,4,16,128]{5,4,3,1,2,0:T(8,128)(2,1)}), bf16[32,2,1,4,16,128]{5,4,3,1,2,0:T(8,128)(2,1)}, u32[]{:S(2)}, u32[]{:S(2)}) async-start(bf16[32,2,1,4,16,128]{5,4,3,1,2,0:T(8,128)(2,1)} %constant_dynamic-update-slice_fusion), calls=%async_computation | async-start | bytes 2097152 | tf_op jit(solution)/shard_map/all_to_all | solution.py:149
  106.9 57.1 %all-reduce.2.cloned.1.call-start = ((), (), s32[]{:S(2)}) async-start(), calls=%async_computation.3 | async-start | bytes 2097152 | tf_op jit(solution)/shard_map/psum | solution.py:119
  108.6 1.5 copy-start.10
  144.7 4.7 %copy-start.8 = (bf16[256,64]{0,1:T(8,128)(2,1)S(1)}, bf16[256,64]{0,1:T(8,128)(2,1)}, u32[]{:S(2)}) copy-start(bf16[256,64]{0,1:T(8,128)(2,1)} %param.25) | copy-start | bytes 98308
  144.7 13.5 %copy-start.5 = (bf16[2048,128]{1,0:T(8,128)(2,1)S(1)}, bf16[2048,128]{1,0:T(8,128)(2,1)}, u32[]{:S(2)}) copy-start(bf16[2048,128]{1,0:T(8,128)(2,1)} %copy-done.4) | copy-start | bytes 1572868
  145.6 21.8 %all-to-all-start.1 = ((bf16[32,4,16,128]{3,2,1,0:T(8,128)(2,1)}), bf16[32,4,16,128]{3,2,1,0:T(8,128)(2,1)S(1)}, u32[]{:S(2)}, u32[]{:S(2)}) async-start(bf16[32,4,16,128]{3,2,1,0:T(8,128)(2,1)} %bitcast.67), calls=%async_computation.1 | async-start | bytes 1048576 | tf_op jit(solution)/shard_map/all_to_all | solution.py:153
  167.9 1.8 %copy-start.3 = (bf16[128,1024]{1,0:T(8,128)(2,1)S(1)}, bf16[128,1024]{1,0:T(8,128)(2,1)}, u32[]{:S(2)}) copy-start(bf16[128,1024]{1,0:T(8,128)(2,1)} %param.28) | copy-start | bytes 786436
  167.9 1.8 %copy-start.13 = (bf16[512,128]{1,0:T(8,128)(2,1)S(1)}, bf16[512,128]{1,0:T(8,128)(2,1)}, u32[]{:S(2)}) copy-start(bf16[512,128]{1,0:T(8,128)(2,1)} %param.29) | copy-start | bytes 393220
  174.0 0.8 copy-start.15
Sparse Core Ops, SparseCore 0:
  14.0 44.1 all-gather.1
  115.1 48.9 all-reduce.1
